TPU v7x, 32 devices: a whole 2x2x4 slice. The times are simulated.
32 devices in a mesh: row: 4 (over x, core), col: 8 (over z, y).
Axes of the slice: x: 2, y: 2, z: 4, core: 2. Of those that a mesh axis runs over, the one named last changes fastest.
Arguments:
- corner: bfloat16 [25600, 25600], P('row', 'col'), may hold values from -32 to 32
- edge: bfloat16 [25600, 25600], P('row', 'col'), may hold values from -32 to 32
- sketch: bfloat16 [25600, 448], P('col'), may hold values from -6 to 6
Outputs:
- corner_new: float32 [400, 400], replicated
- edge_new: float32 [400, 400], replicated
All inputs are finite; a program needn't handle non-finite values.
Results may differ from a plain program's by a relative error of at most 0.0015.
Values may be sent and summed in bfloat16 or wider, within the bound.
A program may use at most 256 MiB of HBM per device.

v0:
```python
import jax
import jax.numpy as jnp
from jax import lax
from jax.sharding import PartitionSpec as P

RANK = 400


def from_root(value, axis, source):
    kept = jnp.where(lax.axis_index(axis) == source, value, 0).astype(value.dtype)
    return lax.psum(kept, axis)


def project(sampled, gram):
    lower = jnp.linalg.cholesky(gram)
    basis = lax.linalg.triangular_solve(
        lower, sampled, left_side=False, lower=True, transpose_a=True
    )
    return basis[:, basis.shape[1] - RANK :].astype(jnp.bfloat16)


def gram_of(sampled):
    return jnp.dot(sampled.T, sampled, precision=lax.Precision.HIGHEST)


def exact_left(narrow_rows, image):
    upper_part = image.astype(jnp.bfloat16)
    lower_part = (image - upper_part.astype(jnp.float32)).astype(jnp.bfloat16)
    first = jnp.dot(narrow_rows.T, upper_part, preferred_element_type=jnp.float32)
    second = jnp.dot(narrow_rows.T, lower_part, preferred_element_type=jnp.float32)
    return first + second


def body(corner, edge, sketch):
    partial_sample = jnp.dot(corner, sketch, preferred_element_type=jnp.float32)
    sampled = lax.psum(partial_sample, "col")
    gram = lax.psum(gram_of(sampled), "row")
    rows_proj = project(sampled, gram)
    width = corner.shape[1]
    ratio = lax.axis_size("col") // lax.axis_size("row")
    col_index = lax.axis_index("col")
    offered = lax.dynamic_slice_in_dim(rows_proj, col_index % ratio * width, width, 0)
    cols_proj = from_root(offered, "row", col_index // ratio)
    corner_part = jnp.dot(corner, cols_proj, preferred_element_type=jnp.float32)
    edge_part = jnp.dot(edge, cols_proj, preferred_element_type=jnp.float32)
    corner_image, edge_image = lax.psum((corner_part, edge_part), "col")
    corner_local = exact_left(rows_proj, corner_image)
    edge_local = exact_left(rows_proj, edge_image)
    corner_new, edge_new = lax.psum((corner_local, edge_local), "row")
    return (corner_new, edge_new)


def solution(mesh):
    placed = (P("row", "col"), P("row", "col"), P("col", None))
    return jax.shard_map(body, mesh=mesh, in_specs=placed, out_specs=(P(), P()), check_vma=False)
```

profile of v0, /device:TPU:0, one launch (start us, length us, event | category | flops | bytes accessed | tf_op | source)
XLA Modules:
  0.0 1422.3 jit_solution(11598771712403457499)
XLA Ops:
  9.0 28.2 %fusion.52 = f32[6400,448]{0,1:T(8,128)} fusion(bf16[6400,3200]{1,0:T(8,128)(2,1)} %param.3, bf16[3200,448]{0,1:T(8,128)(2,1)S(1)} %copy-done), kind=kOutput, calls=%fused_computation.95 | convolution fusion | flops 18350080000 | bytes 55296000 | tf_op jit(solution)/shard_map/dot_general | solution.py:35
  37.3 356.6 %all-reduce.11.cloned.1.call-done = f32[6400,448]{0,1:T(8,128)} async-done(((f32[6400,448]{0,1:T(8,128)}), f32[6400,448]{0,1:T(8,128)}) %all-reduce.11.cloned.1.call-update) | async-done | bytes 11468816 | tf_op jit(solution)/shard_map/psum | solution.py:36
  393.9 22.2 %fusion.53 = f32[448,448]{0,1:T(8,128)} fusion(f32[6400,448]{0,1:T(8,128)} %all-reduce.11.cloned.1.call-done), kind=kOutput, calls=%fused_computation.96 | convolution fusion | flops 15414067200 | bytes 12271616 | tf_op jit(solution)/shard_map/dot_general | solution.py:23
  416.8 34.4 %all-reduce.13.cloned.1.call-done = f32[448,448]{0,1:T(8,128)} async-done(((f32[448,448]{0,1:T(8,128)}), f32[448,448]{0,1:T(8,128)}) %all-reduce.13.cloned.1.call-update) | async-done | bytes 802832 | tf_op jit(solution)/shard_map/psum | solution.py:37
  454.0 11.7 cholesky.105
  465.8 9.8 custom-call.30
  476.3 11.7 cholesky.219
  488.0 9.9 custom-call.31
  498.6 11.7 cholesky.240
  511.1 9.8 custom-call.32
  521.3 5.8 cholesky.260
  531.2 6.0 while.1
  537.3 39.5 %custom-call.33 = f32[4,128,128]{1,2,0:T(8,128)S(1)} custom-call(f32[4,128,128]{2,1,0:T(8,128)S(1)} %pad_maximum_fusion.3), custom_call_target="InvertDiagBlocksLowerTriangular" | custom-call | tf_op jit(solution)/shard_map/triangular_solve | solution.py:16
  576.8 5.1 fusion.51
  582.0 5.3 convolution_subtract_fusion.1
  590.4 6.7 convolution_subtract_fusion
  600.3 7.4 fusion.6
  614.5 59.5 %all-reduce.15.cloned.1.call-done = bf16[3200,400]{0,1:T(8,128)(2,1)} async-done(((bf16[3200,400]{0,1:T(8,128)(2,1)}), bf16[3200,400]{0,1:T(8,128)(2,1)}) %all-reduce.15.cloned.1.call-update) | async-done | bytes 2560016 | tf_op jit(solution)/shard_map/psum | solution.py:11
  674.0 29.0 %convolution_bitcast_fusion.1 = f32[6400,400]{0,1:T(8,128)} fusion(bf16[3200,400]{0,1:T(8,128)(2,1)} %all-reduce.15.cloned.1.call-done, bf16[6400,3200]{1,0:T(8,128)(2,1)} %param.3), kind=kOutput, calls=%fused_computation.3 | convolution fusion | flops 16384000000 | bytes 53760000 | tf_op jit(solution)/shard_map/dot_general | solution.py:44
  703.0 25.5 %convolution_bitcast_fusion = f32[6400,400]{0,1:T(8,128)} fusion(bf16[3200,400]{0,1:T(8,128)(2,1)S(1)} %copy-done.4, bf16[6400,3200]{1,0:T(8,128)(2,1)} %param.4), kind=kOutput, calls=%fused_computation.2 | convolution fusion | flops 16384000000 | bytes 53760000 | tf_op jit(solution)/shard_map/dot_general | solution.py:45
  728.6 613.7 %all-reduce.17.cloned.1.call-done = (f32[6400,400]{0,1:T(8,128)}, f32[6400,400]{0,1:T(8,128)}) async-done(((f32[6400,400]{0,1:T(8,128)}, f32[6400,400]{0,1:T(8,128)}), (f32[6400,400]{0,1:T(8,128)}, f32[6400,400]{0,1:T(8,128)})) %all-reduce.17.cloned.1.call-update) | async-done | bytes 20480016 | tf_op jit(solution)/shard_map/psum | solution.py:46
  1342.3 12.1 fusion.12
  1354.4 7.1 fusion.22
  1368.1 43.2 %all-reduce.19.cloned.1.call-done = (f32[400,400]{1,0:T(8,128)}, f32[400,400]{1,0:T(8,128)}) async-done(((f32[400,400]{1,0:T(8,128)}, f32[400,400]{1,0:T(8,128)}), (f32[400,400]{1,0:T(8,128)}, f32[400,400]{1,0:T(8,128)})) %all-reduce.19.cloned.1.call-update) | async-done | bytes 1280016 | tf_op jit(solution)/shard_map/psum | solution.py:49
  (78 shorter events, 39.2 us)
Async XLA Ops:
  7.2 1.8 copy-start
  7.2 386.7 %all-reduce.11.cloned.1.call-start = ((), (), s32[]{:S(2)}) async-start(), calls=%async_computation | async-start | bytes 22937600 | tf_op jit(solution)/shard_map/psum | solution.py:36
  37.2 413.9 %all-reduce.13.cloned.1.call-start = ((), (), s32[]{:S(2)}) async-start(), calls=%async_computation.1 | async-start | bytes 1835008 | tf_op jit(solution)/shard_map/psum | solution.py:37
  416.1 257.8 %all-reduce.15.cloned.1.call-start = ((), (), s32[]{:S(2)}) async-start(), calls=%async_computation.2 | async-start | bytes 5120000 | tf_op jit(solution)/shard_map/psum | solution.py:11
  610.3 2.2 copy-start.2
  614.5 727.8 %all-reduce.17.cloned.1.call-start = ((), (), s32[]{:S(2)}) async-start(), calls=%async_computation.3 | async-start | bytes 40960000 | tf_op jit(solution)/shard_map/psum | solution.py:46
  674.0 29.0 %copy-start.4 = (bf16[3200,400]{0,1:T(8,128)(2,1)S(1)}, bf16[3200,400]{0,1:T(8,128)(2,1)}, u32[]{:S(2)}) copy-start(bf16[3200,400]{0,1:T(8,128)(2,1)} %all-reduce.15.cloned.1.call-done) | copy-start | bytes 7680004
  728.5 682.8 %all-reduce.19.cloned.1.call-start = ((), (), s32[]{:S(2)}) async-start(), calls=%async_computation.4 | async-start | bytes 3276800 | tf_op jit(solution)/shard_map/psum | solution.py:49
  1342.3 12.1 copy-start.3
  1342.3 19.2 %slice-start = ((s8[5120000]{0:T(1024)(128)(4,1)}), s8[4194304]{0:T(1024)(128)(4,1)S(1)}, s32[]{:S(2)}) async-start(s8[5120000]{0:T(1024)(128)(4,1)} %bitcast.72), calls=%async_computation.5 | async-start | bytes 8388608
  1342.3 19.2 %slice-start.2 = ((s8[10240000]{0:T(1024)(128)(4,1)}), s8[4194304]{0:T(1024)(128)(4,1)S(1)}, s32[]{:S(2)}) async-start(s8[10240000]{0:T(1024)(128)(4,1)} %bitcast.74), calls=%async_computation.7 | async-start | bytes 8388608
  1342.3 19.2 %slice-start.3 = ((s8[10240000]{0:T(1024)(128)(4,1)}), s8[4194304]{0:T(1024)(128)(4,1)S(1)}, s32[]{:S(2)}) async-start(s8[10240000]{0:T(1024)(128)(4,1)} %bitcast.74), calls=%async_computation.8 | async-start | bytes 8388608
  1354.4 7.1 slice-start.1
  1354.4 7.1 slice-start.4
  1364.4 51.1 %copy-start.1 = (bf16[3200,448]{0,1:T(8,128)(2,1)S(1)}, bf16[3200,448]{0,1:T(8,128)(2,1)}, u32[]{:S(2)}) copy-start(bf16[3200,448]{0,1:T(8,128)(2,1)} %param.5) | copy-start | bytes 8601604
Sparse Core Ops, SparseCore 0:
  37.4 356.4 all-reduce.10
  416.3 34.8 all-reduce.12
  614.6 59.3 all-reduce.14
  728.6 613.5 all-reduce.16
  1368.3 43.0 all-reduce.18
where the time goes:
time: 1430 us; the launch traced here: 1420 us
  waiting for transfers between devices  1110 us (78%)
  matrix products  165 us (12%)
  other arithmetic  117 us (8%)
  between operations  17 us (1%)
  local copies, waits for them, and re-layouts  15.8 us (1%)
    psum x1, waiting for transfers between devices, body(): corner_image, edge_image = lax.psum((corner_part, edge_part), 'col')  614 us
    psum x1, waiting for transfers between devices, body(): sampled = lax.psum(partial_sample, 'col')  357 us
    another operation x14, other arithmetic, project(): lower = jnp.linalg.cholesky(gram)  72.7 us
    psum x1, waiting for transfers between devices, from_root(): return lax.psum(kept, axis)  59.5 us
    psum x1, waiting for transfers between devices, body(): corner_new, edge_new = lax.psum((corner_local, edge_local), 'row')  43.2 us
    another operation x8, other arithmetic, project(): lax.linalg.triangular_solve(lower, sampled, left_side=False, lower=True,...  40.7 us
    psum x1, waiting for transfers between devices, body(): gram = lax.psum(gram_of(sampled), 'row')  34.4 us
    another operation x7, matrix products, project(): lax.linalg.triangular_solve(lower, sampled, left_side=False, lower=True,...  32.4 us
  transfers between devices with their start and end apart: 5, of which 5 were waited for; matrix products, arithmetic and copies ran while one was open for 0% of the time, Pallas kernels for 0%

commit v1 on v0

--- a/solution.py
+++ b/solution.py
@@ -33,7 +33,12 @@
 
 def body(corner, edge, sketch):
     partial_sample = jnp.dot(corner, sketch, preferred_element_type=jnp.float32)
-    sampled = lax.psum(partial_sample, "col")
+    cores_n = lax.axis_size("col")
+    sampled = partial_sample
+    for dev in [
+        [(num, num ^ jj) for num in range(cores_n)] for jj in (1, 2, 4, 8, 16) if jj < cores_n
+    ]:
+        sampled = sampled + lax.ppermute(sampled, axis_name="col", perm=dev)
     gram = lax.psum(gram_of(sampled), "row")
     rows_proj = project(sampled, gram)
     width = corner.shape[1]

time: 1430 us -> 2080 us (1.45)
  waiting for transfers between devices: 1110 us -> 1740 us
    ppermute x0 -> x3, waiting for transfers between devices: none -> 984 us  [body(): sampled = sampled + lax.ppermute(sampled, axis_name='col', perm=dev)]
    psum x1 -> x0, waiting for transfers between devices: 357 us -> none  [body(): sampled = lax.psum(partial_sample, 'col')]
  transfers between devices with their start and end apart: 5 -> 7, of which waited for: 5 -> 7; matrix products, arithmetic and copies ran while one was open for 0% -> 0% of each run, Pallas kernels for 0% -> 0%
where the time goes in v1:
time: 2080 us
  waiting for transfers between devices  1740 us (84%)
  matrix products  163 us (8%)
  other arithmetic  132 us (6%)
    ppermute x3, waiting for transfers between devices, body(): sampled = sampled + lax.ppermute(sampled, axis_name='col', perm=dev)  984 us
    psum x1, waiting for transfers between devices, body(): corner_image, edge_image = lax.psum((corner_part, edge_part), 'col')  614 us
    another operation x14, other arithmetic, project(): lower = jnp.linalg.cholesky(gram)  72.7 us
    psum x1, waiting for transfers between devices, from_root(): return lax.psum(kept, axis)  59.5 us
    psum x1, waiting for transfers between devices, body(): corner_new, edge_new = lax.psum((corner_local, edge_local), 'row')  43.2 us
  transfers between devices with their start and end apart: 7, of which 7 were waited for; matrix products, arithmetic and copies ran while one was open for 0% of the time, Pallas kernels for 0%

profile of v1, /device:TPU:0, one launch (start us, length us, event | category | flops | bytes accessed | tf_op | source)
XLA Modules:
  0.0 2076.2 jit_solution(6829279420916596857)
XLA Ops:
  9.0 28.2 %fusion.51 = f32[6400,448]{0,1:T(8,128)} fusion(bf16[6400,3200]{1,0:T(8,128)(2,1)} %param.3, bf16[3200,448]{0,1:T(8,128)(2,1)S(1)} %copy-done), kind=kOutput, calls=%fused_computation.97 | convolution fusion | flops 18350080000 | bytes 55296000 | tf_op jit(solution)/shard_map/dot_general | solution.py:35
  40.2 246.7 %collective-permute-done = f32[6400,448]{0,1:T(8,128)S(1)} collective-permute-done((f32[6400,448]{0,1:T(8,128)}, f32[6400,448]{0,1:T(8,128)S(1)}, u32[]{:S(2)}, u32[]{:S(2)}) %collective-permute-start) | collective-permute-done | bytes 11468832 | tf_op jit(solution)/shard_map/ppermute | solution.py:41
  293.9 246.0 %collective-permute-done.1 = f32[6400,448]{0,1:T(8,128)} collective-permute-done((f32[6400,448]{0,1:T(8,128)S(1)}, f32[6400,448]{0,1:T(8,128)}, u32[]{:S(2)}, u32[]{:S(2)}) %collective-permute-start.1) | collective-permute-done | bytes 11468832 | tf_op jit(solution)/shard_map/ppermute | solution.py:41
  547.6 491.1 %collective-permute-done.2 = f32[6400,448]{0,1:T(8,128)} collective-permute-done((f32[6400,448]{0,1:T(8,128)S(1)}, f32[6400,448]{0,1:T(8,128)}, u32[]{:S(2)}, u32[]{:S(2)}) %collective-permute-start.2) | collective-permute-done | bytes 11468832 | tf_op jit(solution)/shard_map/ppermute | solution.py:41
  1048.1 20.1 fusion.52
  1068.9 36.2 %all-reduce.10.cloned.1.call-done = f32[448,448]{0,1:T(8,128)} async-done(((f32[448,448]{0,1:T(8,128)}), f32[448,448]{0,1:T(8,128)}) %all-reduce.10.cloned.1.call-update) | async-done | bytes 802832 | tf_op jit(solution)/shard_map/psum | solution.py:42
  1107.9 11.7 cholesky.105
  1119.7 9.8 custom-call.30
  1130.2 11.7 cholesky.219
  1142.0 9.9 custom-call.31
  1152.5 11.7 cholesky.240
  1164.9 9.8 custom-call.32
  1175.2 5.8 cholesky.260
  1185.1 6.0 while.1
  1191.2 39.5 %custom-call.33 = f32[4,128,128]{1,2,0:T(8,128)S(1)} custom-call(f32[4,128,128]{2,1,0:T(8,128)S(1)} %pad_maximum_fusion.3), custom_call_target="InvertDiagBlocksLowerTriangular" | custom-call | tf_op jit(solution)/shard_map/triangular_solve | solution.py:16
  1249.0 5.3 fusion.48
  1254.2 5.9 fusion
  1268.5 59.5 %all-reduce.12.cloned.1.call-done = bf16[3200,400]{0,1:T(8,128)(2,1)} async-done(((bf16[3200,400]{0,1:T(8,128)(2,1)}), bf16[3200,400]{0,1:T(8,128)(2,1)}) %all-reduce.12.cloned.1.call-update) | async-done | bytes 2560016 | tf_op jit(solution)/shard_map/psum | solution.py:11
  1327.9 29.1 %convolution_bitcast_fusion.1 = f32[6400,400]{0,1:T(8,128)} fusion(bf16[3200,400]{0,1:T(8,128)(2,1)} %all-reduce.12.cloned.1.call-done, bf16[6400,3200]{1,0:T(8,128)(2,1)} %param.3), kind=kOutput, calls=%fused_computation.3 | convolution fusion | flops 16384000000 | bytes 53760000 | tf_op jit(solution)/shard_map/dot_general | solution.py:49
  1357.0 25.5 %convolution_bitcast_fusion = f32[6400,400]{0,1:T(8,128)} fusion(bf16[3200,400]{0,1:T(8,128)(2,1)S(1)} %copy-done.5, bf16[6400,3200]{1,0:T(8,128)(2,1)} %param.4), kind=kOutput, calls=%fused_computation.2 | convolution fusion | flops 16384000000 | bytes 53760000 | tf_op jit(solution)/shard_map/dot_general | solution.py:50
  1382.6 613.7 %all-reduce.14.cloned.1.call-done = (f32[6400,400]{0,1:T(8,128)}, f32[6400,400]{0,1:T(8,128)}) async-done(((f32[6400,400]{0,1:T(8,128)}, f32[6400,400]{0,1:T(8,128)}), (f32[6400,400]{0,1:T(8,128)}, f32[6400,400]{0,1:T(8,128)})) %all-reduce.14.cloned.1.call-update) | async-done | bytes 20480016 | tf_op jit(solution)/shard_map/psum | solution.py:51
  1996.3 12.1 fusion.10
  2008.4 7.1 fusion.22
  2022.1 43.2 %all-reduce.16.cloned.1.call-done = (f32[400,400]{1,0:T(8,128)}, f32[400,400]{1,0:T(8,128)}) async-done(((f32[400,400]{1,0:T(8,128)}, f32[400,400]{1,0:T(8,128)}), (f32[400,400]{1,0:T(8,128)}, f32[400,400]{1,0:T(8,128)})) %all-reduce.16.cloned.1.call-update) | async-done | bytes 1280016 | tf_op jit(solution)/shard_map/psum | solution.py:54
  (86 shorter events, 79.7 us)
Async XLA Ops:
  7.2 1.8 copy-start
  7.2 1097.8 %all-reduce.10.cloned.1.call-start = ((), (), s32[]{:S(2)}) async-start(), calls=%async_computation | async-start | bytes 1835008 | tf_op jit(solution)/shard_map/psum | solution.py:42
  37.2 249.7 %collective-permute-start = (f32[6400,448]{0,1:T(8,128)}, f32[6400,448]{0,1:T(8,128)S(1)}, u32[]{:S(2)}, u32[]{:S(2)}) collective-permute-start(f32[6400,448]{0,1:T(8,128)} %fusion.51), channel_id=1, source_target_pairs={{0,1},{1,0},{2,3},{3,2},{4,5},{5,4},{6,7},{7,6},{8,9},{9,8},{10,11... | collective-permute-start | bytes 34406408 | tf_op jit(solution)/shard_map/ppermute | solution.py:41
  292.0 247.8 %collective-permute-start.1 = (f32[6400,448]{0,1:T(8,128)S(1)}, f32[6400,448]{0,1:T(8,128)}, u32[]{:S(2)}, u32[]{:S(2)}) collective-permute-start(f32[6400,448]{0,1:T(8,128)S(1)} %add.77), channel_id=1, source_target_pairs={{0,2},{1,3},{2,0},{3,1},{4,6},{5,7},{6,4},{7,5},{8,10},{9,11},{10,... | collective-permute-start | bytes 34406408 | tf_op jit(solution)/shard_map/ppermute | solution.py:41
  545.0 493.6 %collective-permute-start.2 = (f32[6400,448]{0,1:T(8,128)S(1)}, f32[6400,448]{0,1:T(8,128)}, u32[]{:S(2)}, u32[]{:S(2)}) collective-permute-start(f32[6400,448]{0,1:T(8,128)S(1)} %add.78), channel_id=1, source_target_pairs={{0,4},{1,5},{2,6},{3,7},{4,0},{5,1},{6,2},{7,3},{8,12},{9,13},{10,... | collective-permute-start | bytes 34406408 | tf_op jit(solution)/shard_map/ppermute | solution.py:41
  1043.8 4.3 copy-start.2
  1068.2 259.7 %all-reduce.12.cloned.1.call-start = ((), (), s32[]{:S(2)}) async-start(), calls=%async_computation.1 | async-start | bytes 5120000 | tf_op jit(solution)/shard_map/psum | solution.py:11
  1264.2 2.2 copy-start.3
  1268.4 727.9 %all-reduce.14.cloned.1.call-start = ((), (), s32[]{:S(2)}) async-start(), calls=%async_computation.2 | async-start | bytes 40960000 | tf_op jit(solution)/shard_map/psum | solution.py:51
  1327.9 29.1 %copy-start.5 = (bf16[3200,400]{0,1:T(8,128)(2,1)S(1)}, bf16[3200,400]{0,1:T(8,128)(2,1)}, u32[]{:S(2)}) copy-start(bf16[3200,400]{0,1:T(8,128)(2,1)} %all-reduce.12.cloned.1.call-done) | copy-start | bytes 7680004
  1382.5 682.8 %all-reduce.16.cloned.1.call-start = ((), (), s32[]{:S(2)}) async-start(), calls=%async_computation.3 | async-start | bytes 3276800 | tf_op jit(solution)/shard_map/psum | solution.py:54
  1996.3 12.1 copy-start.4
  1996.3 19.2 slice-start
  1996.3 19.2 slice-start.2
  1996.3 19.2 slice-start.3
  2008.4 7.1 slice-start.1
  2008.4 7.1 slice-start.4
  2018.4 51.1 %copy-start.1 = (bf16[3200,448]{0,1:T(8,128)(2,1)S(1)}, bf16[3200,448]{0,1:T(8,128)(2,1)}, u32[]{:S(2)}) copy-start(bf16[3200,448]{0,1:T(8,128)(2,1)} %param.5) | copy-start | bytes 8601604
Sparse Core Ops, SparseCore 0:
  1068.4 36.6 all-reduce.9
  1268.5 59.3 all-reduce.11
  1382.6 613.6 all-reduce.13
  2022.2 43.0 all-reduce.15
